TPU v7x, 32 devices: a whole 2x2x4 slice. The times are simulated.
32 devices in a mesh: plant: 8 (over z, core), col: 4 (over y, x).
Axes of the slice: x: 2, y: 2, z: 4, core: 2. Of those that a mesh axis runs over, the one named last changes fastest.
Arguments:
- tiles: bfloat16 [8, 4, 48, 256, 256], P('plant', 'col'), may hold values from -0.109375 to 0.109375
- tile_row: int32 [8, 4, 48], P('plant', 'col'), may hold values from 0 to 15
- tile_col: int32 [8, 4, 48], P('plant', 'col'), may hold values from 0 to 63
- row_count: int32 [8], P('plant'), may hold values from 2048 to 4096, as said below
- x_start: float32 [32, 65536], P(None, 'col'), may hold values from 0 to 1
- y_start: float32 [32, 32768], P(None, 'plant'), may hold values from 0 to 1
- cost: float32 [65536], P('col'), may hold values from -3 to 3
- upper: float32 [65536], P('col'), may hold values from 0.5 to 2
- demand: float32 [32, 32768], P(None, 'plant'), may hold values from -6 to 6
- tau: float32 [32], replicated, may hold values from 0.2 to 1
- sigma: float32 [32], replicated, may hold values from 0.2 to 1
Outputs:
- primal: float32 [32, 65536], P(None, 'col')
- dual: float32 [32, 32768], P(None, 'plant')
Inputs may be any that keep to these rules, and one draw needn't show every extreme that they name: Each plant block has row_count live rows, the first ones of its block; at least one plant block is full. `tile_row`: tiles at the same position add up.
All inputs are finite; a program needn't handle non-finite values.
Results may differ from a plain program's by a relative error of at most 0.003.
Values sent between devices are 32-bit elements; how exact they have to be, the bound alone decides.
No kernel may reach another device: no remote copies, remote signals or barrier semaphores. Data moves between devices by JAX's collectives and lax.ppermute only.
A program may use at most 64 MiB of HBM per device.

v0:
```python
import jax
import jax.numpy as jnp
from jax import lax
from jax.sharding import PartitionSpec as P

ITERS = 3


def body(tiles, tile_row, tile_col, row_count, x_start, y_start, cost, upper, demand, tau, sigma):
    blocks = tiles[0, 0]
    rows = tile_row[0, 0]
    cols = tile_col[0, 0]
    tile_width = blocks.shape[1]
    scenarios, rows_dev = y_start.shape
    col_width = x_start.shape[1]
    row_tiles = rows_dev // tile_width
    col_tiles = col_width // tile_width
    live = (jnp.arange(rows_dev, dtype=jnp.int32) < row_count[0]).astype(jnp.float32)[None, :]
    row_hot = (jnp.arange(row_tiles, dtype=jnp.int32)[:, None] == rows[None, :]).astype(jnp.float32)
    col_hot = (jnp.arange(col_tiles, dtype=jnp.int32)[:, None] == cols[None, :]).astype(jnp.float32)
    step_primal = tau[:, None]
    step_dual = sigma[:, None]
    cost_row = cost[None, :]
    upper_row = upper[None, :]
    primal = x_start
    dual = y_start * live
    for iteration in range(ITERS):
        dual_low = dual.astype(jnp.bfloat16).reshape(scenarios, row_tiles, tile_width)
        picked = jnp.take(dual_low, rows, axis=1)
        contrib = jnp.einsum("str,trc->stc", picked, blocks, preferred_element_type=jnp.float32)
        kty_part = jnp.einsum(
            "kt,stc->skc", col_hot, contrib, precision=lax.Precision.HIGHEST
        ).reshape(scenarios, col_width)
        kty = lax.psum(kty_part, "plant")
        primal_new = jnp.minimum(
            jnp.maximum(primal - step_primal * (cost_row - kty), 0.0), upper_row
        )
        extra = (
            (2.0 * primal_new - primal)
            .astype(jnp.bfloat16)
            .reshape(scenarios, col_tiles, tile_width)
        )
        chosen = jnp.take(extra, cols, axis=1)
        product = jnp.einsum("stc,trc->str", chosen, blocks, preferred_element_type=jnp.float32)
        kx_part = jnp.einsum(
            "kt,str->skr", row_hot, product, precision=lax.Precision.HIGHEST
        ).reshape(scenarios, rows_dev)
        kx = lax.psum(kx_part, "col")
        dual = jnp.maximum(dual + step_dual * (demand - kx), 0.0) * live
        primal = primal_new
    return (primal, dual)


def solution(mesh):
    placed = (
        P("plant", "col", None, None, None),
        P("plant", "col", None),
        P("plant", "col", None),
        P("plant"),
        P(None, "col"),
        P(None, "plant"),
        P("col"),
        P("col"),
        P(None, "plant"),
        P(),
        P(),
    )
    return jax.shard_map(
        body,
        mesh=mesh,
        in_specs=placed,
        out_specs=(P(None, "col"), P(None, "plant")),
        check_vma=False,
    )
```

profile of v0, /device:TPU:0, one launch (start us, length us, event | category | flops | bytes accessed | tf_op | source)
XLA Modules:
  0.0 428.5 jit_solution(13103330824339237959)
XLA Ops:
  11.0 4.0 fusion.24
  15.0 2.1 fusion.22
  17.1 2.5 copy.31
  19.8 67.6 %all-reduce.7.cloned.1.call-done = f32[32,16384]{1,0:T(8,128)} async-done(((f32[32,16384]{1,0:T(8,128)}), f32[32,16384]{1,0:T(8,128)}) %all-reduce.7.cloned.1.call-update) | async-done | bytes 2097168 | tf_op jit(solution)/shard_map/psum | solution.py:34
  87.4 2.2 subtract_convert_fusion.2
  90.7 1.8 gather_fusion.1
  92.6 4.7 %fusion.27 = f32[32,48,256]{2,0,1:T(8,128)S(1)} fusion(bf16[1,1,48,256,256]{4,3,2,1,0:T(8,128)(2,1)} %param.15, bf16[48,32,256]{2,1,0:T(8,128)(2,1)S(1)} %gather_fusion.1, pred[48]{0:T(512)(128)(4,1)S(1)} %compare_and_fusion), kind=kOutput, calls=%fused_computation.37 | convolution fusion | flops 201719808 | bytes 8650800 | tf_op jit(solution)/shard_map/stc,trc->str/dot_general | solution.py:44
  100.2 44.9 %all-reduce.9.cloned.1.call-done = f32[32,4096]{1,0:T(8,128)} async-done(((f32[32,4096]{1,0:T(8,128)}), f32[32,4096]{1,0:T(8,128)}) %all-reduce.9.cloned.1.call-update) | async-done | bytes 524304 | tf_op jit(solution)/shard_map/psum | solution.py:48
  148.1 4.3 fusion.30
  152.4 2.2 fusion.18
  154.5 2.5 copy.33
  157.1 65.0 %all-reduce.11.cloned.1.call-done = f32[32,16384]{1,0:T(8,128)} async-done(((f32[32,16384]{1,0:T(8,128)}), f32[32,16384]{1,0:T(8,128)}) %all-reduce.11.cloned.1.call-update) | async-done | bytes 2097168 | tf_op jit(solution)/shard_map/psum | solution.py:34
  222.1 3.1 subtract_convert_fusion.1
  226.4 2.9 gather_fusion.3
  229.3 5.0 %fusion.33 = f32[32,48,256]{2,0,1:T(8,128)S(1)} fusion(bf16[1,1,48,256,256]{4,3,2,1,0:T(8,128)(2,1)} %param.15, bf16[48,32,256]{2,1,0:T(8,128)(2,1)} %gather_fusion.3, pred[48]{0:T(512)(128)(4,1)S(1)} %copy-done.12), kind=kOutput, calls=%fused_computation.39 | convolution fusion | flops 201719808 | bytes 8650800 | tf_op jit(solution)/shard_map/stc,trc->str/dot_general | solution.py:44
  237.2 44.9 %all-reduce.13.cloned.1.call-done = f32[32,4096]{1,0:T(8,128)} async-done(((f32[32,4096]{1,0:T(8,128)}), f32[32,4096]{1,0:T(8,128)}) %all-reduce.13.cloned.1.call-update) | async-done | bytes 524304 | tf_op jit(solution)/shard_map/psum | solution.py:48
  285.2 4.3 fusion.36
  289.5 2.1 fusion.14
  291.6 2.5 copy.35
  294.3 65.0 %all-reduce.15.cloned.1.call-done = f32[32,16384]{1,0:T(8,128)} async-done(((f32[32,16384]{1,0:T(8,128)}), f32[32,16384]{1,0:T(8,128)}) %all-reduce.15.cloned.1.call-update) | async-done | bytes 2097168 | tf_op jit(solution)/shard_map/psum | solution.py:34
  359.3 5.4 %subtract_convert_fusion = (bf16[32,16384]{1,0:T(8,128)(2,1)S(1)}, f32[32,16384]{1,0:T(8,128)}) fusion(f32[32,16384]{1,0:T(8,128)} %all-reduce.11.cloned.1.call-done, f32[16384]{0:T(1024)S(1)} %copy-done.4, f32[32,16384]{1,0:T(8,128)S(1)} %copy-done, f32[32,16384]{1,0:T(8,128)} %all-reduce.7.cloned.1.call-done, f32[16384]{0:T(1024)S(1)} %copy-done.5, ...), kind=kLoop, calls=%fused_computation.18 | loop fusion | flops 9437184 | bytes 11665536 | tf_op jit(solution)/shard_map/convert_element_type | solution.py:40
  366.5 5.0 %fusion.39 = f32[32,48,256]{2,0,1:T(8,128)S(1)} fusion(bf16[1,1,48,256,256]{4,3,2,1,0:T(8,128)(2,1)} %param.15, bf16[48,32,256]{2,1,0:T(8,128)(2,1)} %gather_fusion.5, pred[48]{0:T(512)(128)(4,1)S(1)} %copy-done.13), kind=kOutput, calls=%fused_computation.41 | convolution fusion | flops 201719808 | bytes 8650800 | tf_op jit(solution)/shard_map/stc,trc->str/dot_general | solution.py:44
  374.2 45.1 %all-reduce.17.cloned.1.call-done = f32[32,4096]{1,0:T(8,128)} async-done(((f32[32,4096]{1,0:T(8,128)}), f32[32,4096]{1,0:T(8,128)}) %all-reduce.17.cloned.1.call-update) | async-done | bytes 524304 | tf_op jit(solution)/shard_map/psum | solution.py:48
  419.3 2.3 maximum_multiply_fusion
  (86 shorter events, 21.8 us)
Async XLA Ops:
  7.2 80.3 %all-reduce.7.cloned.1.call-start = ((), (), s32[]{:S(2)}) async-start(), calls=%async_computation | async-start | bytes 4194304 | tf_op jit(solution)/shard_map/psum | solution.py:34
  7.9 7.1 %copy-start.14 = (pred[48]{0:T(512)(128)(4,1)}, pred[48]{0:T(512)(128)(4,1)S(1)}, u32[]{:S(2)}) copy-start(pred[48]{0:T(512)(128)(4,1)S(1)} %compare_and_fusion.1) | copy-start | bytes 148
  9.2 5.8 %copy-start.7 = (s32[1024]{0:T(1024)}, s32[1024]{0:T(1024)S(1)}, u32[]{:S(2)}) copy-start(s32[1024]{0:T(1024)S(1)} %pad_clamp_fusion.1) | copy-start | bytes 12292
  17.1 70.3 %copy-start.4 = (f32[16384]{0:T(1024)S(1)}, f32[16384]{0:T(1024)}, u32[]{:S(2)}) copy-start(f32[16384]{0:T(1024)} %param.22) | copy-start | bytes 196612
  17.1 70.3 %copy-start.5 = (f32[16384]{0:T(1024)S(1)}, f32[16384]{0:T(1024)}, u32[]{:S(2)}) copy-start(f32[16384]{0:T(1024)} %param.21) | copy-start | bytes 196612
  19.7 67.8 %copy-start = (f32[32,16384]{1,0:T(8,128)S(1)}, f32[32,16384]{1,0:T(8,128)}, u32[]{:S(2)}) copy-start(f32[32,16384]{1,0:T(8,128)} %param.19) | copy-start | bytes 6291460
  19.7 67.8 %copy-start.18 = (f32[32]{0:T(128)S(1)}, f32[32]{0:T(128)}, u32[]{:S(2)}) copy-start(f32[32]{0:T(128)} %param.24) | copy-start | bytes 388
  19.7 125.4 %all-reduce.9.cloned.1.call-start = ((), (), s32[]{:S(2)}) async-start(), calls=%async_computation.1 | async-start | bytes 1048576 | tf_op jit(solution)/shard_map/psum | solution.py:48
  19.8 70.9 %copy-start.6 = (s32[1024]{0:T(1024)}, s32[1024]{0:T(1024)S(1)}, u32[]{:S(2)}) copy-start(s32[1024]{0:T(1024)S(1)} %pad_clamp_fusion) | copy-start | bytes 12292
  19.8 72.8 %copy-start.11 = (pred[48]{0:T(512)(128)(4,1)}, pred[48]{0:T(512)(128)(4,1)S(1)}, u32[]{:S(2)}) copy-start(pred[48]{0:T(512)(128)(4,1)S(1)} %compare_and_fusion) | copy-start | bytes 148
  97.3 47.8 %copy-start.1 = (f32[32,4096]{1,0:T(8,128)S(1)}, f32[32,4096]{1,0:T(8,128)}, u32[]{:S(2)}) copy-start(f32[32,4096]{1,0:T(8,128)} %param.20) | copy-start | bytes 1572868
  97.3 47.8 %copy-start.2 = (f32[32,4096]{1,0:T(8,128)S(1)}, f32[32,4096]{1,0:T(8,128)}, u32[]{:S(2)}) copy-start(f32[32,4096]{1,0:T(8,128)} %param.23) | copy-start | bytes 1572868
  97.3 47.8 %copy-start.15 = (f32[32]{0:T(128)S(1)}, f32[32]{0:T(128)}, u32[]{:S(2)}) copy-start(f32[32]{0:T(128)} %param.25) | copy-start | bytes 388
  100.0 122.1 %all-reduce.11.cloned.1.call-start = ((), (), s32[]{:S(2)}) async-start(), calls=%async_computation.2 | async-start | bytes 4194304 | tf_op jit(solution)/shard_map/psum | solution.py:34
  157.0 65.1 %copy-start.19 = (f32[32]{0:T(128)S(1)}, f32[32]{0:T(128)}, u32[]{:S(2)}) copy-start(f32[32]{0:T(128)} %param.24) | copy-start | bytes 388
  157.1 125.0 %all-reduce.13.cloned.1.call-start = ((), (), s32[]{:S(2)}) async-start(), calls=%async_computation.3 | async-start | bytes 1048576 | tf_op jit(solution)/shard_map/psum | solution.py:48
  229.3 5.0 %copy-start.9 = (s32[1,1,48]{2,1,0:T(1,128)S(1)}, s32[1,1,48]{2,1,0:T(1,128)}, u32[]{:S(2)}) copy-start(s32[1,1,48]{2,1,0:T(1,128)} %param.16) | copy-start | bytes 580
  234.3 47.8 %copy-start.16 = (f32[32]{0:T(128)S(1)}, f32[32]{0:T(128)}, u32[]{:S(2)}) copy-start(f32[32]{0:T(128)} %param.25) | copy-start | bytes 388
  236.9 122.3 %all-reduce.15.cloned.1.call-start = ((), (), s32[]{:S(2)}) async-start(), calls=%async_computation.4 | async-start | bytes 4194304 | tf_op jit(solution)/shard_map/psum | solution.py:34
  294.2 65.1 %copy-start.20 = (f32[32]{0:T(128)S(1)}, f32[32]{0:T(128)}, u32[]{:S(2)}) copy-start(f32[32]{0:T(128)} %param.24) | copy-start | bytes 388
  294.2 125.1 %all-reduce.17.cloned.1.call-start = ((), (), s32[]{:S(2)}) async-start(), calls=%async_computation.5 | async-start | bytes 1048576 | tf_op jit(solution)/shard_map/psum | solution.py:48
  366.5 5.0 %copy-start.10 = (s32[1,1,48]{2,1,0:T(1,128)S(1)}, s32[1,1,48]{2,1,0:T(1,128)}, u32[]{:S(2)}) copy-start(s32[1,1,48]{2,1,0:T(1,128)} %param.16) | copy-start | bytes 580
  371.5 47.8 %copy-start.3 = (f32[32,4096]{1,0:T(8,128)S(1)}, f32[32,4096]{1,0:T(8,128)}, u32[]{:S(2)}) copy-start(f32[32,4096]{1,0:T(8,128)} %all-reduce.9.cloned.1.call-done) | copy-start | bytes 1572868
  371.5 47.8 %copy-start.17 = (f32[32]{0:T(128)S(1)}, f32[32]{0:T(128)}, u32[]{:S(2)}) copy-start(f32[32]{0:T(128)} %param.25) | copy-start | bytes 388
  (6 other events, 23.1 us)
Sparse Core Ops, SparseCore 0:
  19.8 67.5 all-reduce.6
  100.1 44.9 all-reduce.8
  157.2 64.8 all-reduce.10
  237.1 44.9 all-reduce.12
  294.3 64.8 all-reduce.14
  374.3 44.9 all-reduce.16
where the time goes:
time: 429 us; the launch traced here: 428 us
  waiting for transfers between devices  333 us (78%)
  matrix products  38.2 us (9%)
  local copies, waits for them, and re-layouts  23.7 us (6%)
  other arithmetic  18.2 us (4%)
  between operations  15.1 us (4%)
    psum x3, waiting for transfers between devices, body(): kty = lax.psum(kty_part, 'plant')  198 us
    psum x3, waiting for transfers between devices, body(): kx = lax.psum(kx_part, 'col')  135 us
    dot_general x3, matrix products, body(): jnp.einsum('stc,trc->str', chosen, blocks, preferred_element_type=jnp.flo...  14.7 us
    dot_general x3, matrix products, body(): jnp.einsum('str,trc->stc', picked, blocks, preferred_element_type=jnp.flo...  12.5 us
    unnamed x54, local copies, waits for them, and re-layouts  11 us
    convert_element_type x3, other arithmetic, body(): extra = (2.0 * primal_new - primal).astype(jnp.bfloat16).reshape(scenario...  10.7 us
  transfers between devices with their start and end apart: 6, of which 6 were waited for; matrix products, arithmetic and copies ran while one was open for 0% of the time, Pallas kernels for 0%

commit v1 on v0

--- a/solution.py
+++ b/solution.py
@@ -31,7 +31,9 @@
         kty_part = jnp.einsum(
             "kt,stc->skc", col_hot, contrib, precision=lax.Precision.HIGHEST
         ).reshape(scenarios, col_width)
-        kty = lax.psum(kty_part, "plant")
+        kty = kty_part
+        for hop in (1, 2, 4):
+            kty = kty + lax.ppermute(kty, "plant", [(dev, dev ^ hop) for dev in range(8)])
         primal_new = jnp.minimum(
             jnp.maximum(primal - step_primal * (cost_row - kty), 0.0), upper_row
         )

time: 429 us -> 655 us (1.53)
  waiting for transfers between devices: 333 us -> 558 us
  starting transfers between devices: 0.65 us -> 15.1 us
  local copies, waits for them, and re-layouts: 23.7 us -> 15.5 us
    ppermute x0 -> x9, waiting for transfers between devices: none -> 421 us  [body(): lax.ppermute(kty, 'plant', [(dev, dev ^ hop) for dev in range(8)])]
    psum x3 -> x0, waiting for transfers between devices: 198 us -> none  [body(): kty = lax.psum(kty_part, 'plant')]
    ppermute x0 -> x9, starting transfers between devices: none -> 14.5 us  [body(): lax.ppermute(kty, 'plant', [(dev, dev ^ hop) for dev in range(8)])]
  transfers between devices with their start and end apart: 6 -> 12, of which waited for: 6 -> 12; matrix products, arithmetic and copies ran while one was open for 0% -> 0% of each run, Pallas kernels for 0% -> 0%
where the time goes in v1:
time: 655 us; the launch traced here: 654 us
  waiting for transfers between devices  558 us (85%)
  matrix products  37.6 us (6%)
  local copies, waits for them, and re-layouts  15.5 us (2%)
  starting transfers between devices  15.1 us (2%)
  between operations  14.9 us (2%)
  other arithmetic  13.2 us (2%)
    ppermute x9, waiting for transfers between devices, body(): lax.ppermute(kty, 'plant', [(dev, dev ^ hop) for dev in range(8)])  421 us
    psum x3, waiting for transfers between devices, body(): kx = lax.psum(kx_part, 'col')  137 us
    ppermute x9, starting transfers between devices, body(): lax.ppermute(kty, 'plant', [(dev, dev ^ hop) for dev in range(8)])  14.5 us
    dot_general x3, matrix products, body(): jnp.einsum('stc,trc->str', chosen, blocks, preferred_element_type=jnp.flo...  14.4 us
  transfers between devices with their start and end apart: 12, of which 12 were waited for; matrix products, arithmetic and copies ran while one was open for 0% of the time, Pallas kernels for 0%

profile of v1, /device:TPU:0, one launch (start us, length us, event | category | flops | bytes accessed | tf_op | source)
XLA Modules:
  0.0 654.5 jit_solution(18034267396256187678)
XLA Ops:
  11.0 4.0 fusion.24
  18.9 3.8 collective-permute-done
  22.9 3.0 collective-permute-start.1
  25.9 45.9 %collective-permute-done.1 = f32[32,16384]{1,0:T(8,128)S(1)} collective-permute-done((f32[32,16384]{1,0:T(8,128)S(1)}, f32[32,16384]{1,0:T(8,128)S(1)}, u32[]{:S(2)}, u32[]{:S(2)}) %collective-permute-start.1) | collective-permute-done | bytes 2097184 | tf_op jit(solution)/shard_map/ppermute | solution.py:36
  72.1 2.8 collective-permute-start.2
  74.9 90.2 %collective-permute-done.2 = f32[32,16384]{1,0:T(8,128)S(1)} collective-permute-done((f32[32,16384]{1,0:T(8,128)S(1)}, f32[32,16384]{1,0:T(8,128)S(1)}, u32[]{:S(2)}, u32[]{:S(2)}) %collective-permute-start.2) | collective-permute-done | bytes 2097184 | tf_op jit(solution)/shard_map/ppermute | solution.py:36
  168.0 4.7 fusion.27
  175.6 46.3 %all-reduce.4.cloned.1.call-done = f32[32,4096]{1,0:T(8,128)} async-done(((f32[32,4096]{1,0:T(8,128)}), f32[32,4096]{1,0:T(8,128)}) %all-reduce.4.cloned.1.call-update) | async-done | bytes 524304 | tf_op jit(solution)/shard_map/psum | solution.py:50
  223.8 4.0 fusion.30
  231.2 4.1 collective-permute-done.3
  237.2 46.2 %collective-permute-done.4 = f32[32,16384]{1,0:T(8,128)S(1)} collective-permute-done((f32[32,16384]{1,0:T(8,128)S(1)}, f32[32,16384]{1,0:T(8,128)S(1)}, u32[]{:S(2)}, u32[]{:S(2)}) %collective-permute-start.4) | collective-permute-done | bytes 2097184 | tf_op jit(solution)/shard_map/ppermute | solution.py:36
  283.6 2.5 collective-permute-start.5
  286.0 90.3 %collective-permute-done.5 = f32[32,16384]{1,0:T(8,128)S(1)} collective-permute-done((f32[32,16384]{1,0:T(8,128)S(1)}, f32[32,16384]{1,0:T(8,128)S(1)}, u32[]{:S(2)}, u32[]{:S(2)}) %collective-permute-start.5) | collective-permute-done | bytes 2097184 | tf_op jit(solution)/shard_map/ppermute | solution.py:36
  378.1 2.8 gather_fusion.3
  380.9 5.0 fusion.33
  388.8 45.2 %all-reduce.6.cloned.1.call-done = f32[32,4096]{1,0:T(8,128)} async-done(((f32[32,4096]{1,0:T(8,128)}), f32[32,4096]{1,0:T(8,128)}) %all-reduce.6.cloned.1.call-update) | async-done | bytes 524304 | tf_op jit(solution)/shard_map/psum | solution.py:50
  437.1 4.3 fusion.36
  444.9 4.1 collective-permute-done.6
  450.8 46.2 %collective-permute-done.7 = f32[32,16384]{1,0:T(8,128)S(1)} collective-permute-done((f32[32,16384]{1,0:T(8,128)S(1)}, f32[32,16384]{1,0:T(8,128)S(1)}, u32[]{:S(2)}, u32[]{:S(2)}) %collective-permute-start.7) | collective-permute-done | bytes 2097184 | tf_op jit(solution)/shard_map/ppermute | solution.py:36
  497.2 2.5 collective-permute-start.8
  499.7 90.3 %collective-permute-done.8 = f32[32,16384]{1,0:T(8,128)S(1)} collective-permute-done((f32[32,16384]{1,0:T(8,128)S(1)}, f32[32,16384]{1,0:T(8,128)S(1)}, u32[]{:S(2)}, u32[]{:S(2)}) %collective-permute-start.8) | collective-permute-done | bytes 2097184 | tf_op jit(solution)/shard_map/ppermute | solution.py:36
  592.9 4.7 fusion.39
  600.3 45.5 %all-reduce.8.cloned.1.call-done = f32[32,4096]{1,0:T(8,128)} async-done(((f32[32,4096]{1,0:T(8,128)}), f32[32,4096]{1,0:T(8,128)}) %all-reduce.8.cloned.1.call-update) | async-done | bytes 524304 | tf_op jit(solution)/shard_map/psum | solution.py:50
  645.8 2.2 maximum_multiply_fusion
  (95 shorter events, 39.2 us)
Async XLA Ops:
  7.2 214.7 %all-reduce.4.cloned.1.call-start = ((), (), s32[]{:S(2)}) async-start(), calls=%async_computation | async-start | bytes 1048576 | tf_op jit(solution)/shard_map/psum | solution.py:50
  7.9 215.9 %copy-start.16 = (pred[48]{0:T(512)(128)(4,1)}, pred[48]{0:T(512)(128)(4,1)S(1)}, u32[]{:S(2)}) copy-start(pred[48]{0:T(512)(128)(4,1)S(1)} %compare_and_fusion.1) | copy-start | bytes 148
  9.2 213.9 %copy-start.9 = (s32[1024]{0:T(1024)}, s32[1024]{0:T(1024)S(1)}, u32[]{:S(2)}) copy-start(s32[1024]{0:T(1024)S(1)} %pad_clamp_fusion.1) | copy-start | bytes 12292
  18.4 4.3 collective-permute-start
  22.9 142.3 %copy-start.4 = (f32[32,16384]{1,0:T(8,128)S(1)}, f32[32,16384]{1,0:T(8,128)}, u32[]{:S(2)}) copy-start(f32[32,16384]{1,0:T(8,128)} %param.19) | copy-start | bytes 6291460
  22.9 142.3 %copy-start.6 = (f32[16384]{0:T(1024)S(1)}, f32[16384]{0:T(1024)}, u32[]{:S(2)}) copy-start(f32[16384]{0:T(1024)} %param.22) | copy-start | bytes 196612
  22.9 142.2 %copy-start.7 = (f32[16384]{0:T(1024)S(1)}, f32[16384]{0:T(1024)}, u32[]{:S(2)}) copy-start(f32[16384]{0:T(1024)} %param.21) | copy-start | bytes 196612
  22.9 142.2 %copy-start.10 = (f32[32]{0:T(128)S(1)}, f32[32]{0:T(128)}, u32[]{:S(2)}) copy-start(f32[32]{0:T(128)} %param.24) | copy-start | bytes 388
  22.9 48.9 %collective-permute-start.1 = (f32[32,16384]{1,0:T(8,128)S(1)}, f32[32,16384]{1,0:T(8,128)S(1)}, u32[]{:S(2)}, u32[]{:S(2)}) collective-permute-start(f32[32,16384]{1,0:T(8,128)S(1)} %add.54), channel_id=1, source_target_pairs={{0,8},{4,12},{8,0},{12,4},{16,24},{20,28},{24,16},{28,20},{1,9},{5... | collective-permute-start | bytes 6291464 | tf_op jit(solution)/shard_map/ppermute | solution.py:36
  72.1 93.1 %collective-permute-start.2 = (f32[32,16384]{1,0:T(8,128)S(1)}, f32[32,16384]{1,0:T(8,128)S(1)}, u32[]{:S(2)}, u32[]{:S(2)}) collective-permute-start(f32[32,16384]{1,0:T(8,128)S(1)} %add.55), channel_id=1, source_target_pairs={{0,16},{4,20},{8,24},{12,28},{16,0},{20,4},{24,8},{28,12},{1,17},{... | collective-permute-start | bytes 6291464 | tf_op jit(solution)/shard_map/ppermute | solution.py:36
  74.9 303.2 %copy-start.8 = (s32[1024]{0:T(1024)}, s32[1024]{0:T(1024)S(1)}, u32[]{:S(2)}) copy-start(s32[1024]{0:T(1024)S(1)} %pad_clamp_fusion) | copy-start | bytes 12292
  74.9 306.0 %copy-start.14 = (pred[48]{0:T(512)(128)(4,1)}, pred[48]{0:T(512)(128)(4,1)S(1)}, u32[]{:S(2)}) copy-start(pred[48]{0:T(512)(128)(4,1)S(1)} %compare_and_fusion) | copy-start | bytes 148
  172.7 49.2 %copy-start.1 = (f32[32,4096]{1,0:T(8,128)S(1)}, f32[32,4096]{1,0:T(8,128)}, u32[]{:S(2)}) copy-start(f32[32,4096]{1,0:T(8,128)} %param.20) | copy-start | bytes 1572868
  172.7 49.2 %copy-start.2 = (f32[32,4096]{1,0:T(8,128)S(1)}, f32[32,4096]{1,0:T(8,128)}, u32[]{:S(2)}) copy-start(f32[32,4096]{1,0:T(8,128)} %param.23) | copy-start | bytes 1572868
  175.4 258.6 %all-reduce.6.cloned.1.call-start = ((), (), s32[]{:S(2)}) async-start(), calls=%async_computation.1 | async-start | bytes 1048576 | tf_op jit(solution)/shard_map/psum | solution.py:50
  231.2 4.2 collective-permute-start.3
  235.6 140.7 %copy-start = (f32[32,16384]{1,0:T(8,128)S(1)}, f32[32,16384]{1,0:T(8,128)}, u32[]{:S(2)}) copy-start(f32[32,16384]{1,0:T(8,128)} %get-tuple-element.9) | copy-start | bytes 6291460
  235.6 47.7 %collective-permute-start.4 = (f32[32,16384]{1,0:T(8,128)S(1)}, f32[32,16384]{1,0:T(8,128)S(1)}, u32[]{:S(2)}, u32[]{:S(2)}) collective-permute-start(f32[32,16384]{1,0:T(8,128)S(1)} %add.58), channel_id=1, source_target_pairs={{0,8},{4,12},{8,0},{12,4},{16,24},{20,28},{24,16},{28,20},{1,9},{5... | collective-permute-start | bytes 6291464 | tf_op jit(solution)/shard_map/ppermute | solution.py:36
  283.6 92.7 %collective-permute-start.5 = (f32[32,16384]{1,0:T(8,128)S(1)}, f32[32,16384]{1,0:T(8,128)S(1)}, u32[]{:S(2)}, u32[]{:S(2)}) collective-permute-start(f32[32,16384]{1,0:T(8,128)S(1)} %add.59), channel_id=1, source_target_pairs={{0,16},{4,20},{8,24},{12,28},{16,0},{20,4},{24,8},{28,12},{1,17},{... | collective-permute-start | bytes 6291464 | tf_op jit(solution)/shard_map/ppermute | solution.py:36
  388.5 257.2 %all-reduce.8.cloned.1.call-start = ((), (), s32[]{:S(2)}) async-start(), calls=%async_computation.2 | async-start | bytes 1048576 | tf_op jit(solution)/shard_map/psum | solution.py:50
  444.8 4.2 collective-permute-start.6
  449.2 140.7 %copy-start.11 = (f32[32]{0:T(128)S(1)}, f32[32]{0:T(128)}, u32[]{:S(2)}) copy-start(f32[32]{0:T(128)} %param.24) | copy-start | bytes 388
  449.2 47.7 %collective-permute-start.7 = (f32[32,16384]{1,0:T(8,128)S(1)}, f32[32,16384]{1,0:T(8,128)S(1)}, u32[]{:S(2)}, u32[]{:S(2)}) collective-permute-start(f32[32,16384]{1,0:T(8,128)S(1)} %add.62), channel_id=1, source_target_pairs={{0,8},{4,12},{8,0},{12,4},{16,24},{20,28},{24,16},{28,20},{1,9},{5... | collective-permute-start | bytes 6291464 | tf_op jit(solution)/shard_map/ppermute | solution.py:36
  497.2 92.7 %collective-permute-start.8 = (f32[32,16384]{1,0:T(8,128)S(1)}, f32[32,16384]{1,0:T(8,128)S(1)}, u32[]{:S(2)}, u32[]{:S(2)}) collective-permute-start(f32[32,16384]{1,0:T(8,128)S(1)} %add.63), channel_id=1, source_target_pairs={{0,16},{4,20},{8,24},{12,28},{16,0},{20,4},{24,8},{28,12},{1,17},{... | collective-permute-start | bytes 6291464 | tf_op jit(solution)/shard_map/ppermute | solution.py:36
  (9 other events, 212.3 us)
Sparse Core Ops, SparseCore 0:
  175.5 46.3 all-reduce.3
  388.6 45.3 all-reduce.5
  600.4 45.3 all-reduce.7
